TPU v7x, 32 devices: a whole 2x2x4 slice. The times are simulated.
32 devices in a mesh: gx: 4 (over z), gy: 2 (over core), gz: 4 (over y, x).
Axes of the slice: x: 2, y: 2, z: 4, core: 2. Of those that a mesh axis runs over, the one named last changes fastest.
Arguments:
- tokens: bfloat16 [16384, 768], P(('gx', 'gy', 'gz')), may hold values from -6 to 6
- segment_ids: int32 [8, 2048], P(('gx', 'gy')), may hold values from 0 to 15, never falling along the last dimension, each value on 1 to 1024 neighbouring positions
- valid_mask: int32 [8, 2048], P(('gx', 'gy')), may hold values from 0 to 1, as said below
- cotangent: bfloat16 [16384, 768], P(('gx', 'gy', 'gz')), may hold values from -6 to 6
- teacher: bfloat16 [16384, 768], P(('gx', 'gy', 'gz')), may hold values from -6 to 6
- w_query: bfloat16 [768, 768], P('gy', 'gz'), may hold values from -0.21875 to 0.21875
- b_query: bfloat16 [768], P('gz'), may hold values from -3 to 3
- w_key: bfloat16 [768, 768], P('gy', 'gz'), may hold values from -0.21875 to 0.21875
- w_value: bfloat16 [768, 768], P('gy', 'gz'), may hold values from -0.21875 to 0.21875
- b_value: bfloat16 [768], P('gz'), may hold values from -0.5 to 0.5
- w_out: bfloat16 [768, 768], P('gz', 'gy'), may hold values from -1.75 to 1.75
- b_out: bfloat16 [768], replicated, may hold values from -1.1953125 to 1.1953125
- norm1_gain: bfloat16 [768], replicated, may hold values from 0.5 to 1.5
- norm1_bias: bfloat16 [768], replicated, may hold values from -1.1953125 to 1.1953125
- w_up: bfloat16 [768, 3072], P('gy', 'gz'), may hold values from -0.21875 to 0.21875
- b_up: bfloat16 [3072], P('gz'), may hold values from -3 to 3
- w_down: bfloat16 [3072, 768], P('gz', 'gy'), may hold values from -0.109375 to 0.109375
- b_down: bfloat16 [768], replicated, may hold values from -1.1953125 to 1.1953125
- norm2_gain: bfloat16 [768], replicated, may hold values from 0.5 to 1.5
- norm2_bias: bfloat16 [768], replicated, may hold values from -1.1953125 to 1.1953125
Outputs:
- output: bfloat16 [16384, 768], P(('gx', 'gy', 'gz'))
- mean_loss: float32 [], replicated
- d_tokens: bfloat16 [16384, 768], P(('gx', 'gy', 'gz'))
- d_w_query: float32 [768, 768], P('gy', 'gz')
- d_b_query: float32 [768], P('gz')
- d_w_key: float32 [768, 768], P('gy', 'gz')
- d_w_value: float32 [768, 768], P('gy', 'gz')
- d_b_value: float32 [768], P('gz')
- d_w_out: float32 [768, 768], P('gz', 'gy')
- d_b_out: float32 [768], replicated
- d_norm1_gain: float32 [768], replicated
- d_norm1_bias: float32 [768], replicated
- d_w_up: float32 [768, 3072], P('gy', 'gz')
- d_b_up: float32 [3072], P('gz')
- d_w_down: float32 [3072, 768], P('gz', 'gy')
- d_b_down: float32 [768], replicated
- d_norm2_gain: float32 [768], replicated
- d_norm2_bias: float32 [768], replicated
Inputs may be any that keep to these rules, and one draw needn't show every extreme that they name: `segment_ids`: within a sequence the ids never fall, and each id that occurs forms one run of 1 to 1024 positions. `valid_mask`: in each sequence the valid tokens are a leading run of 512 positions or more, padding after it.
All inputs are finite; a program needn't handle non-finite values.
Results may differ from a plain program's by a relative error of at most 0.02.
Values may be sent and summed in bfloat16 or wider, within the bound.
No kernel may reach another device: no remote copies, remote signals or barrier semaphores. Data moves between devices by JAX's collectives and lax.ppermute only.
A program may use at most 128 MiB of HBM per device.

v0:
```python
import math
import jax
import jax.numpy as jnp
from jax import lax
from jax.sharding import PartitionSpec as P

HEAD = 64
MASKED = -1e30
EPSILON = 1e-05


def gather_rows(tensor):
    return lax.all_gather(tensor, "gz", axis=0, tiled=True)


def sum_rows(term_fn, row_count):
    return lax.psum_scatter(
        term_fn(jnp.int32(0), lax.axis_size("gz") * row_count).astype(jnp.bfloat16),
        "gz",
        scatter_dimension=0,
        tiled=True,
    ).astype(jnp.float32)


def norm_forward(resid, gain, shift):
    average = jnp.mean(resid, -1, keepdims=True)
    centered = resid - average
    inv_std = lax.rsqrt(jnp.mean(centered * centered, -1, keepdims=True) + EPSILON)
    normed = centered * inv_std
    return (normed * gain + shift, normed, inv_std)


def norm_backward(upstream, normed, inv_std, gain):
    d_gain = jnp.sum(upstream * normed, 0)
    d_shift = jnp.sum(upstream, 0)
    scaled = upstream * gain
    d_resid = inv_std * (
        scaled
        - jnp.mean(scaled, -1, keepdims=True)
        - normed * jnp.mean(scaled * normed, -1, keepdims=True)
    )
    return (d_resid, d_gain, d_shift)


def gelu_parts(preact):
    normal_cdf = 0.5 * (1.0 + lax.erf(preact * (1.0 / math.sqrt(2.0))))
    slope = normal_cdf + preact * jnp.exp(-0.5 * preact * preact) * (1.0 / math.sqrt(2.0 * math.pi))
    return (preact * normal_cdf, slope)


def allowed_block(seg_row, valid_row, first_row, block_rows):
    query_pos = first_row + jnp.arange(block_rows, dtype=jnp.int32)
    key_pos = jnp.arange(seg_row.shape[0], dtype=jnp.int32)
    query_seg = lax.dynamic_slice_in_dim(seg_row, first_row, block_rows)
    return (query_seg[:, None] == seg_row[None, :]) & (
        (valid_row[None, :] == 1) | (query_pos[:, None] == key_pos[None, :])
    )


def attention_forward(queries, key_rows, value_rows, seg_row, valid_row, block_rows):
    length, col_width = queries.shape
    head_count = col_width // HEAD
    score_scale = HEAD ** (-0.5)

    def one_block(block_index):
        first_row = block_index * block_rows
        allowed = allowed_block(seg_row, valid_row, first_row, block_rows)
        query_block = lax.dynamic_slice_in_dim(queries, first_row, block_rows)
        outputs = []
        log_parts = []
        for head_index in range(head_count):
            columns = slice(head_index * HEAD, (head_index + 1) * HEAD)
            scores = (
                jnp.einsum(
                    "qd,kd->qk",
                    query_block[:, columns],
                    key_rows[:, columns],
                    preferred_element_type=jnp.float32,
                )
                * score_scale
            )
            scores = jnp.where(allowed, scores, MASKED)
            row_max = jnp.max(scores, -1, keepdims=True)
            weights = jnp.exp(scores - row_max)
            exp_total = jnp.sum(weights, -1, keepdims=True)
            probs_low = (weights / exp_total).astype(jnp.bfloat16)
            outputs.append(
                jnp.dot(probs_low, value_rows[:, columns], preferred_element_type=jnp.float32)
            )
            log_parts.append((row_max + jnp.log(exp_total))[:, 0])
        return (jnp.concatenate(outputs, 1), jnp.stack(log_parts, 1))

    outputs, log_sums = lax.map(one_block, jnp.arange(length // block_rows, dtype=jnp.int32))
    return (outputs.reshape(length, col_width), log_sums.reshape(length, head_count))


def attention_backward(
    queries, key_rows, value_rows, d_attended, log_sums, seg_row, valid_row, block_rows
):
    length, col_width = queries.shape
    head_count = col_width // HEAD
    score_scale = HEAD ** (-0.5)

    def one_block(carried, block_index):
        d_key_sum, d_value_sum = carried
        first_row = block_index * block_rows
        allowed = allowed_block(seg_row, valid_row, first_row, block_rows)
        query_block = lax.dynamic_slice_in_dim(queries, first_row, block_rows)
        grad_block = lax.dynamic_slice_in_dim(d_attended, first_row, block_rows)
        log_block = lax.dynamic_slice_in_dim(log_sums, first_row, block_rows)
        query_parts = []
        key_parts = []
        value_parts = []
        for head_index in range(head_count):
            columns = slice(head_index * HEAD, (head_index + 1) * HEAD)
            scores = (
                jnp.einsum(
                    "qd,kd->qk",
                    query_block[:, columns],
                    key_rows[:, columns],
                    preferred_element_type=jnp.float32,
                )
                * score_scale
            )
            scores = jnp.where(allowed, scores, MASKED)
            probs = jnp.exp(scores - log_block[:, head_index : head_index + 1])
            d_probs = jnp.einsum(
                "qd,kd->qk",
                grad_block[:, columns],
                value_rows[:, columns],
                preferred_element_type=jnp.float32,
            )
            d_scores = (probs * (d_probs - jnp.sum(probs * d_probs, -1, keepdims=True))).astype(
                jnp.bfloat16
            )
            query_parts.append(
                jnp.dot(d_scores, key_rows[:, columns], preferred_element_type=jnp.float32)
                * score_scale
            )
            key_parts.append(
                jnp.einsum(
                    "qk,qd->kd",
                    d_scores,
                    query_block[:, columns],
                    preferred_element_type=jnp.float32,
                )
                * score_scale
            )
            value_parts.append(
                jnp.einsum(
                    "qk,qd->kd",
                    probs.astype(jnp.bfloat16),
                    grad_block[:, columns],
                    preferred_element_type=jnp.float32,
                )
            )
        d_key_sum = d_key_sum + jnp.concatenate(key_parts, 1)
        d_value_sum = d_value_sum + jnp.concatenate(value_parts, 1)
        return ((d_key_sum, d_value_sum), jnp.concatenate(query_parts, 1))

    zero_rows = jnp.zeros((length, col_width), jnp.float32)
    (d_key_sum, d_value_sum), d_query_blocks = lax.scan(
        one_block, (zero_rows, zero_rows), jnp.arange(length // block_rows, dtype=jnp.int32)
    )
    return (d_query_blocks.reshape(length, col_width), d_key_sum, d_value_sum)


def shards(
    tokens,
    segment_ids,
    valid_mask,
    cotangent,
    teacher,
    w_query,
    b_query,
    w_key,
    w_value,
    b_value,
    w_out,
    b_out,
    norm1_gain,
    norm1_bias,
    w_up,
    b_up,
    w_down,
    b_down,
    norm2_gain,
    norm2_bias,
):
    row_count = tokens.shape[0]
    group_rows = row_count * lax.axis_size("gz")
    block_rows = min(512, group_rows)
    own_first = lax.axis_index("gz") * row_count
    seg_row = segment_ids[0]
    valid_row = valid_mask[0]
    own_valid = lax.dynamic_slice_in_dim(valid_row, own_first, row_count).astype(jnp.float32)[
        :, None
    ]
    query_cols, key_cols, value_cols, up_cols = (
        lax.all_gather(w_query, "gy", axis=0, tiled=True),
        lax.all_gather(w_key, "gy", axis=0, tiled=True),
        lax.all_gather(w_value, "gy", axis=0, tiled=True),
        lax.all_gather(w_up, "gy", axis=0, tiled=True),
    )
    out_rows, down_rows = (
        lax.all_gather(w_out, "gy", axis=1, tiled=True),
        lax.all_gather(w_down, "gy", axis=1, tiled=True),
    )
    col_width = query_cols.shape[1]
    qkv_weight = jnp.concatenate([query_cols, key_cols, value_cols], 1)
    qkv_bias = jnp.concatenate(
        [
            b_query.astype(jnp.float32),
            jnp.zeros((col_width,), jnp.float32),
            b_value.astype(jnp.float32),
        ]
    )
    tokens_all = gather_rows(tokens)
    projected = (
        jnp.dot(tokens_all, qkv_weight, preferred_element_type=jnp.float32) + qkv_bias
    ).astype(jnp.bfloat16)
    queries = projected[:, :col_width]
    key_rows = projected[:, col_width : 2 * col_width]
    value_rows = projected[:, 2 * col_width :]
    attended, log_sums = attention_forward(
        queries, key_rows, value_rows, seg_row, valid_row, block_rows
    )
    attended = attended.astype(jnp.bfloat16)

    def out_term(first_row, span_rows):
        return jnp.dot(
            lax.dynamic_slice_in_dim(attended, first_row, span_rows),
            out_rows,
            preferred_element_type=jnp.float32,
        )

    mixed_rows = sum_rows(out_term, row_count) + b_out.astype(jnp.float32)
    resid1 = tokens.astype(jnp.float32) + mixed_rows
    hidden, normed1, inv_std1 = norm_forward(
        resid1, norm1_gain.astype(jnp.float32), norm1_bias.astype(jnp.float32)
    )
    hidden_low = hidden.astype(jnp.bfloat16)
    hidden_all = gather_rows(hidden_low)
    preact = jnp.dot(hidden_all, up_cols, preferred_element_type=jnp.float32) + b_up.astype(
        jnp.float32
    )
    activated, slope = gelu_parts(preact)
    activated = activated.astype(jnp.bfloat16)

    def down_term(first_row, span_rows):
        return jnp.dot(
            lax.dynamic_slice_in_dim(activated, first_row, span_rows),
            down_rows,
            preferred_element_type=jnp.float32,
        )

    branch = sum_rows(down_term, row_count)
    resid2 = hidden + (branch + b_down.astype(jnp.float32))
    norm2_gain_f = norm2_gain.astype(jnp.float32)
    output_full, normed2, inv_std2 = norm_forward(
        resid2, norm2_gain_f, norm2_bias.astype(jnp.float32)
    )
    mismatch = output_full - teacher.astype(jnp.float32)
    error_part = jnp.sum(own_valid * mismatch * mismatch)
    count_part = jnp.sum(own_valid)
    d_output = cotangent.astype(jnp.float32) + own_valid * mismatch
    d_resid2, d_norm2_gain, d_norm2_bias = norm_backward(d_output, normed2, inv_std2, norm2_gain_f)
    d_branch = d_resid2.astype(jnp.bfloat16)
    d_b_down = jnp.sum(d_branch, 0, dtype=jnp.float32)
    d_branch_all = gather_rows(d_branch)
    d_act = jnp.einsum("lm,fm->lf", d_branch_all, down_rows, preferred_element_type=jnp.float32)
    d_down = jnp.einsum("lf,lm->fm", activated, d_branch_all, preferred_element_type=jnp.float32)
    d_pre = (d_act * slope).astype(jnp.bfloat16)
    d_bias_up = jnp.sum(d_pre, 0, dtype=jnp.float32)
    d_up = jnp.einsum("lm,lf->mf", hidden_all, d_pre, preferred_element_type=jnp.float32)

    def back_term(first_row, span_rows):
        return jnp.einsum(
            "lf,mf->lm",
            lax.dynamic_slice_in_dim(d_pre, first_row, span_rows),
            up_cols,
            preferred_element_type=jnp.float32,
        )

    d_hidden = d_resid2 + sum_rows(back_term, row_count)
    d_resid1, d_norm1_gain, d_norm1_bias = norm_backward(
        d_hidden, normed1, inv_std1, norm1_gain.astype(jnp.float32)
    )
    d_mixed = d_resid1.astype(jnp.bfloat16)
    d_b_out = jnp.sum(d_mixed, 0, dtype=jnp.float32)
    d_mixed_all = gather_rows(d_mixed)
    d_attended = jnp.einsum(
        "lm,cm->lc", d_mixed_all, out_rows, preferred_element_type=jnp.float32
    ).astype(jnp.bfloat16)
    d_out_w = jnp.einsum("lc,lm->cm", attended, d_mixed_all, preferred_element_type=jnp.float32)
    d_query_rows, d_key_rows, d_value_rows = attention_backward(
        queries, key_rows, value_rows, d_attended, log_sums, seg_row, valid_row, block_rows
    )
    d_projected = jnp.concatenate([d_query_rows, d_key_rows, d_value_rows], 1).astype(jnp.bfloat16)
    d_qkv_w = jnp.einsum("lm,lc->mc", tokens_all, d_projected, preferred_element_type=jnp.float32)
    d_bias_qkv = jnp.sum(d_projected, 0, dtype=jnp.float32)

    def input_term(first_row, span_rows):
        return jnp.einsum(
            "lc,mc->lm",
            lax.dynamic_slice_in_dim(d_projected, first_row, span_rows),
            qkv_weight,
            preferred_element_type=jnp.float32,
        )

    d_tokens = d_resid1 + sum_rows(input_term, row_count)
    grad_query, grad_key, grad_value, grad_up = (
        lax.psum_scatter(
            d_qkv_w[:, :col_width].astype(jnp.bfloat16), "gy", scatter_dimension=0, tiled=True
        ).astype(jnp.float32),
        lax.psum_scatter(
            d_qkv_w[:, col_width : 2 * col_width].astype(jnp.bfloat16),
            "gy",
            scatter_dimension=0,
            tiled=True,
        ).astype(jnp.float32),
        lax.psum_scatter(
            d_qkv_w[:, 2 * col_width :].astype(jnp.bfloat16), "gy", scatter_dimension=0, tiled=True
        ).astype(jnp.float32),
        lax.psum_scatter(d_up.astype(jnp.bfloat16), "gy", scatter_dimension=0, tiled=True).astype(
            jnp.float32
        ),
    )
    grad_out, grad_down = (
        lax.psum_scatter(
            d_out_w.astype(jnp.bfloat16), "gy", scatter_dimension=1, tiled=True
        ).astype(jnp.float32),
        lax.psum_scatter(d_down.astype(jnp.bfloat16), "gy", scatter_dimension=1, tiled=True).astype(
            jnp.float32
        ),
    )
    grad_query, grad_key, grad_value, grad_up, grad_out, grad_down = (
        lax.psum(grad_query.astype(jnp.bfloat16), "gx").astype(jnp.float32),
        lax.psum(grad_key.astype(jnp.bfloat16), "gx").astype(jnp.float32),
        lax.psum(grad_value.astype(jnp.bfloat16), "gx").astype(jnp.float32),
        lax.psum(grad_up.astype(jnp.bfloat16), "gx").astype(jnp.float32),
        lax.psum(grad_out.astype(jnp.bfloat16), "gx").astype(jnp.float32),
        lax.psum(grad_down.astype(jnp.bfloat16), "gx").astype(jnp.float32),
    )
    grad_b_query, grad_b_value, grad_b_up = lax.psum(
        (d_bias_qkv[:col_width], d_bias_qkv[2 * col_width :], d_bias_up), ("gx", "gy")
    )
    (
        grad_gain1,
        grad_shift1,
        grad_gain2,
        grad_shift2,
        grad_b_out,
        grad_b_down,
        error_sum,
        count_sum,
    ) = lax.psum(
        (
            d_norm1_gain,
            d_norm1_bias,
            d_norm2_gain,
            d_norm2_bias,
            d_b_out,
            d_b_down,
            error_part,
            count_part,
        ),
        ("gx", "gy", "gz"),
    )
    mean_loss = error_sum / (count_sum * tokens.shape[1])
    return (
        output_full.astype(jnp.bfloat16),
        mean_loss,
        d_tokens.astype(jnp.bfloat16),
        grad_query,
        grad_b_query,
        grad_key,
        grad_value,
        grad_b_value,
        grad_out,
        grad_b_out,
        grad_gain1,
        grad_shift1,
        grad_up,
        grad_b_up,
        grad_down,
        grad_b_down,
        grad_gain2,
        grad_shift2,
    )


def solution(mesh):
    placed = (
        P(("gx", "gy", "gz"), None),
        P(("gx", "gy"), None),
        P(("gx", "gy"), None),
        P(("gx", "gy", "gz"), None),
        P(("gx", "gy", "gz"), None),
        P("gy", "gz"),
        P("gz"),
        P("gy", "gz"),
        P("gy", "gz"),
        P("gz"),
        P("gz", "gy"),
        P(),
        P(),
        P(),
        P("gy", "gz"),
        P("gz"),
        P("gz", "gy"),
        P(),
        P(),
        P(),
    )
    return jax.shard_map(
        shards,
        mesh=mesh,
        in_specs=placed,
        out_specs=(
            P(("gx", "gy", "gz"), None),
            P(),
            P(("gx", "gy", "gz"), None),
            P("gy", "gz"),
            P("gz"),
            P("gy", "gz"),
            P("gy", "gz"),
            P("gz"),
            P("gz", "gy"),
            P(),
            P(),
            P(),
            P("gy", "gz"),
            P("gz"),
            P("gz", "gy"),
            P(),
            P(),
            P(),
        ),
        check_vma=False,
    )
```

profile of v0, /device:TPU:0, one launch (start us, length us, event | category | flops | bytes accessed | tf_op | source)
XLA Modules:
  0.0 751.6 jit_solution(14504390201831847154)
XLA Ops:
  10.1 2.4 all_gather.34
  12.5 2.3 all_gather.30
  14.8 2.3 all_gather.31
  17.1 2.3 all_gather.32
  19.5 37.9 %all-gather.7.cloned.1.call-done = bf16[2048,768]{1,0:T(8,128)(2,1)} async-done(((bf16[512,768]{1,0:T(8,128)(2,1)}), bf16[2048,768]{1,0:T(8,128)(2,1)}) %all-gather.7.cloned.1.call-update) | async-done | bytes 3145744 | tf_op jit(solution)/shard_map/all_gather | solution.py:13
  57.4 3.9 fusion.63
  66.1 52.2 %while.27 = (s32[]{:T(128)}, bf16[4,512,192]{1,2,0:T(8,128)(2,1)}, f32[4,512,3]{1,2,0:T(4,128)S(1)}, s32[4]{0:T(128)S(1)}, s32[2048]{0:T(1024)S(1)}, /*index=5*/...) while((s32[]{:T(128)}, bf16[4,512,192]{1,2,0:T(8,128)(2,1)}, ...), condition=%wide.region_7.8_spmd, body=%wide.region_0.7_spmd.sunk | while | flops 843649024 | bytes 42000656 | solution.py:93
  67.4 1.9 fusion.158
  71.2 1.8 fusion.155
  80.5 1.9 fusion.158
  84.3 1.8 fusion.155
  93.5 1.9 fusion.158
  97.3 1.8 fusion.155
  100.9 1.8 fusion.161
  106.6 1.9 fusion.158
  110.4 1.8 fusion.155
  120.8 2.7 convolution_convert_fusion.3
  124.6 43.0 %reduce-scatter.21.cloned.1.call-done = bf16[512,768]{1,0:T(8,128)(2,1)} async-done(((bf16[2048,768]{1,0:T(8,128)(2,1)}), bf16[512,768]{1,0:T(8,128)(2,1)}) %reduce-scatter.21.cloned.1.call-update) | async-done | bytes 786448 | tf_op jit(solution)/shard_map/reduce_scatter | solution.py:17
  172.9 43.2 %all-gather.9.cloned.1.call-done = bf16[2048,768]{1,0:T(8,128)(2,1)} async-done(((bf16[512,768]{1,0:T(8,128)(2,1)}), bf16[2048,768]{1,0:T(8,128)(2,1)}) %all-gather.9.cloned.1.call-update) | async-done | bytes 3145744 | tf_op jit(solution)/shard_map/all_gather | solution.py:13
  216.1 7.0 multiply_convert_fusion.3
  223.0 3.6 all-gather.13.cloned.1.call-done
  226.6 6.5 convolution_convert_fusion.1
  234.4 43.8 %reduce-scatter.23.cloned.1.call-done = bf16[512,768]{1,0:T(8,128)(2,1)} async-done(((bf16[2048,768]{1,0:T(8,128)(2,1)}), bf16[512,768]{1,0:T(8,128)(2,1)}) %reduce-scatter.23.cloned.1.call-update) | async-done | bytes 786448 | tf_op jit(solution)/shard_map/reduce_scatter | solution.py:17
  278.2 2.3 fusion.69
  281.4 2.9 fusion.71
  284.3 3.0 convert_reduce_fusion.2
  287.4 44.1 %all-gather.15.cloned.1.call-done = bf16[2048,768]{1,0:T(8,128)(2,1)} async-done(((bf16[512,768]{1,0:T(8,128)(2,1)}), bf16[2048,768]{1,0:T(8,128)(2,1)}) %all-gather.15.cloned.1.call-update) | async-done | bytes 3145744 | tf_op jit(solution)/shard_map/all_gather | solution.py:13
  331.5 8.1 %convert_reduce_fusion = (f32[768]{0:T(1024)}, bf16[2048,768]{1,0:T(8,128)(2,1)S(1)}) fusion(f32[2048,768]{1,0:T(8,128)} %get-tuple-element.364, f32[768]{0:T(1024)S(1)} %convert_element_type.207, bf16[2048,768]{1,0:T(8,128)(2,1)} %all-gather.15.cloned.1.call-done, bf16[768,768]{1,0:T(8,128)(2,1)} %all-gather.13.cloned.1.call-done), kind=kOutput, calls=%fused_computation.103 | convolution fusion | flops 2436365568 | bytes 13768704 | tf_op jit(solution)/shard_map/lm,fm->lf/dot_general | solution.py:271
  341.2 4.0 convolution_convert_fusion
  345.3 43.9 %reduce-scatter.25.cloned.1.call-done = bf16[512,768]{1,0:T(8,128)(2,1)} async-done(((bf16[2048,768]{1,0:T(8,128)(2,1)}), bf16[512,768]{1,0:T(8,128)(2,1)}) %reduce-scatter.25.cloned.1.call-update) | async-done | bytes 786448 | tf_op jit(solution)/shard_map/reduce_scatter | solution.py:17
  389.2 3.5 multiply_reduce_fusion.4
  392.8 2.8 convert_reduce_fusion.3
  395.6 5.5 convolution_convert_fusion.5
  402.7 37.0 %all-gather.17.cloned.1.call-done = bf16[2048,768]{1,0:T(8,128)(2,1)} async-done(((bf16[512,768]{1,0:T(8,128)(2,1)}), bf16[2048,768]{1,0:T(8,128)(2,1)}) %all-gather.17.cloned.1.call-update) | async-done | bytes 3145744 | tf_op jit(solution)/shard_map/all_gather | solution.py:13
  439.7 4.0 convolution_convert_fusion.4
  444.6 106.6 %while.28 = (s32[]{:T(128)}, f32[2048,192]{0,1:T(8,128)}, f32[2048,192]{0,1:T(8,128)}, bf16[4,512,192]{1,2,0:T(8,128)(2,1)}, s32[4]{0:T(128)S(1)}, /*index=5*/s3...) while((s32[]{:T(128)}, f32[2048,192]{0,1:T(8,128)}, ...), condition=%wide.region_27.28_spmd.clone, body=%wide.region_23.27_spmd.clone.sunk | while | flops 2058486784 | bytes 141845040 | solution.py:162
  451.2 2.4 multiply_reduce_fusion.14
  456.7 2.5 multiply_reduce_fusion.15
  462.5 2.4 multiply_reduce_fusion.16
  477.8 2.4 multiply_reduce_fusion.14
  483.2 2.5 multiply_reduce_fusion.15
  489.1 2.4 multiply_reduce_fusion.16
  504.3 2.4 multiply_reduce_fusion.14
  509.8 2.5 multiply_reduce_fusion.15
  515.6 2.4 multiply_reduce_fusion.16
  530.9 2.4 multiply_reduce_fusion.14
  536.4 2.5 multiply_reduce_fusion.15
  542.2 2.4 multiply_reduce_fusion.16
  551.3 2.1 copy.80
  553.4 2.7 convolution_convert_fusion.8
  557.0 2.5 convert.16
  560.6 4.4 fusion.67
  568.0 6.5 convolution_convert_fusion.6
  574.7 2.2 copy.74
  581.0 9.4 %reduce-scatter.33.cloned.1.call-done = bf16[384,192]{1,0:T(8,128)(2,1)} async-done(((bf16[768,192]{1,0:T(8,128)(2,1)}), bf16[384,192]{1,0:T(8,128)(2,1)}) %reduce-scatter.33.cloned.1.call-update) | async-done | bytes 147472
  592.2 9.5 %reduce-scatter.31.cloned.1.call-done = bf16[384,192]{1,0:T(8,128)(2,1)} async-done(((bf16[768,192]{1,0:T(8,128)(2,1)}), bf16[384,192]{1,0:T(8,128)(2,1)}) %reduce-scatter.31.cloned.1.call-update) | async-done | bytes 147472
  603.3 10.9 %reduce-scatter.29.cloned.1.call-done = bf16[384,768]{1,0:T(8,128)(2,1)} async-done(((bf16[768,768]{1,0:T(8,128)(2,1)}), bf16[384,768]{1,0:T(8,128)(2,1)}) %reduce-scatter.29.cloned.1.call-update) | async-done | bytes 589840 | tf_op jit(solution)/shard_map/reduce_scatter | solution.py:325
  614.3 5.2 convolution_convert_fusion.2
  620.3 43.8 %all-reduce = (f32[]{:T(128)}, f32[]{:T(128)}, f32[768]{0:T(1024)}, f32[768]{0:T(1024)}, f32[768]{0:T(1024)}, /*index=5*/f32[768]{0:T(1024)}, f32[768]{0:T(1024)}, f32[768]{0:T(1024)}) all-reduce(f32[]{:T(128)} %get-tuple-element.262, f32[]{:T(128)} %get-tuple-element.334, ...), channel_id=1, replica_groups=mesh['gx'=4,'gy'=2,'gz'=4] {'gx','gy','gz'}, use_global_device_ids=true, to_apply=%region_15.16 | all-reduce | flops 4610 | bytes 36880 | tf_op jit(solution)/shard_map/psum | solution.py:357
  665.7 16.3 %all-reduce.1 = (f32[192]{0:T(256)}, f32[192]{0:T(256)}, f32[768]{0:T(1024)}) all-reduce(f32[192]{0:T(256)S(1)} %get-tuple-element.362, f32[192]{0:T(256)S(1)} %get-tuple-element.361, f32[768]{0:T(1024)S(1)} %copy-done.33), channel_id=1, replica_groups=mesh['gx'=4,'gy'=2,'gz'=4] {'gx','gy'}, use_global_device_ids=true, to_apply=%region_32.33 | all-reduce | flops 1152 | bytes 9216 | tf_op jit(solution)/shard_map/psum | solution.py:345
  682.0 12.6 %all-reduce.5.cloned.1.call-done = (bf16[384,192]{0,1:T(8,128)(2,1)}, bf16[384,192]{0,1:T(8,128)(2,1)}, bf16[384,192]{0,1:T(8,128)(2,1)}, bf16[192,384]{1,0:T(8,...) async-done(((bf16[384,192]{0,1:T(8,128)(2,1)}, bf16[384,192]{0,1:T(8,128)(2,1)}, bf16[384,192]{0,1:T(8,128)(2,1)}, bf16[192,384]{1,0:T(8,128)(2,1)}, ...) | async-done | bytes 1769488 | tf_op jit(solution)/shard_map/psum | solution.py:338
  701.4 2.2 convert_element_type.236
  704.6 35.9 %reduce-scatter.27.cloned.1.call-done = bf16[512,768]{1,0:T(8,128)(2,1)} async-done(((bf16[2048,768]{1,0:T(8,128)(2,1)}), bf16[512,768]{1,0:T(8,128)(2,1)}) %reduce-scatter.27.cloned.1.call-update) | async-done | bytes 786448 | tf_op jit(solution)/shard_map/reduce_scatter | solution.py:17
  740.5 2.2 add_convert_fusion.1
  (361 shorter events, 151.0 us)
Async XLA Ops:
  8.0 49.4 %all-gather.7.cloned.1.call-start = ((), (), s32[]{:S(2)}) async-start(), calls=%async_computation.10 | async-start | bytes 3932160 | tf_op jit(solution)/shard_map/all_gather | solution.py:13
  8.8 158.9 %reduce-scatter.21.cloned.1.call-start = ((), (), s32[]{:S(2)}) async-start(), calls=%async_computation.11 | async-start | bytes 3932160 | tf_op jit(solution)/shard_map/reduce_scatter | solution.py:17
  12.5 107.3 %copy-start.22 = (bf16[192,768]{1,0:T(8,128)(2,1)}, bf16[192,768]{1,0:T(8,128)(2,1)S(1)}, u32[]{:S(2)}) copy-start(bf16[192,768]{1,0:T(8,128)(2,1)S(1)} %all_gather.34) | copy-start | bytes 884740
  19.5 37.9 %copy-start.25 = (bf16[768,576]{0,1:T(8,128)(2,1)}, bf16[768,576]{0,1:T(8,128)(2,1)S(1)}, u32[]{:S(2)}) copy-start(bf16[768,576]{0,1:T(8,128)(2,1)S(1)} %constant_dynamic-update-slice_fusion) | copy-start | bytes 2654212
  63.1 2.9 copy-start.23
  63.1 2.9 copy-start.26
  118.2 1.6 copy-start.12
  123.5 1.1 copy-start.35
  123.5 1.1 copy-start.36
  123.5 44.2 %copy-start = (bf16[512,768]{1,0:T(8,128)(2,1)S(1)}, bf16[512,768]{1,0:T(8,128)(2,1)}, u32[]{:S(2)}) copy-start(bf16[512,768]{1,0:T(8,128)(2,1)} %param.24) | copy-start | bytes 2359300
  123.5 49.3 %all-gather.11.cloned.1.call-start = ((), (), s32[]{:S(2)}) async-start(), calls=%async_computation.13 | async-start | bytes 1769472 | tf_op jit(solution)/shard_map/all_gather | solution.py:203
  124.1 91.9 %all-gather.9.cloned.1.call-start = ((), (), s32[]{:S(2)}) async-start(), calls=%async_computation.12 | async-start | bytes 3932160 | tf_op jit(solution)/shard_map/all_gather | solution.py:13
  167.7 3.1 copy-start.6
  169.2 3.6 copy-start.37
  172.2 54.4 %all-gather.13.cloned.1.call-start = ((), (), s32[]{:S(2)}) async-start(), calls=%async_computation.14 | async-start | bytes 1769472 | tf_op jit(solution)/shard_map/all_gather | solution.py:207
  172.8 105.5 %reduce-scatter.23.cloned.1.call-start = ((), (), s32[]{:S(2)}) async-start(), calls=%async_computation.15 | async-start | bytes 3932160 | tf_op jit(solution)/shard_map/reduce_scatter | solution.py:17
  233.1 98.4 %all-gather.15.cloned.1.call-start = ((), (), s32[]{:S(2)}) async-start(), calls=%async_computation.16 | async-start | bytes 3932160 | tf_op jit(solution)/shard_map/all_gather | solution.py:13
  278.2 2.3 copy-start.7
  278.2 2.3 copy-start.14
  278.2 3.2 copy-start.17
  278.2 3.2 copy-start.18
  287.4 101.8 %reduce-scatter.25.cloned.1.call-start = ((), (), s32[]{:S(2)}) async-start(), calls=%async_computation.17 | async-start | bytes 3932160 | tf_op jit(solution)/shard_map/reduce_scatter | solution.py:17
  331.5 9.7 %copy-start.41 = (bf16[768,768]{1,0:T(8,128)(2,1)S(1)}, bf16[768,768]{1,0:T(8,128)(2,1)}, u32[]{:S(2)}) copy-start(bf16[768,768]{1,0:T(8,128)(2,1)} %all-gather.11.cloned.1.call-done) | copy-start | bytes 3538948
  339.6 1.7 copy-start.42
  345.3 94.4 %all-gather.17.cloned.1.call-start = ((), (), s32[]{:S(2)}) async-start(), calls=%async_computation.18 | async-start | bytes 3932160 | tf_op jit(solution)/shard_map/all_gather | solution.py:13
  389.2 3.6 copy-start.8
  389.2 3.6 copy-start.9
  389.2 3.6 copy-start.21
  395.6 179.1 %reduce-scatter.39.cloned.1.call-start = ((), (), s32[]{:S(2)}) async-start(), calls=%async_computation.25 | async-start | bytes 1769472
  402.6 174.3 %reduce-scatter.37.cloned.1.call-start = ((), (), s32[]{:S(2)}) async-start(), calls=%async_computation.24 | async-start | bytes 589824
  444.6 108.7 %copy-start.11 = (bf16[4,24,8,512]{3,2,0,1:T(8,128)(2,1)S(1)}, bf16[4,24,8,512]{3,2,0,1:T(8,128)(2,1)}, u32[]{:S(2)}) copy-start(bf16[4,24,8,512]{3,2,0,1:T(8,128)(2,1)} %copy-done.10) | copy-start | bytes 2359300
  449.5 1.7 copy-start.13
  466.7 1.4 copy-start.1
  466.7 1.9 copy-start.4
  469.6 1.3 copy-start.2
  469.7 1.7 copy-start.5
  476.1 1.7 copy-start.13
  493.2 1.4 copy-start.1
  493.2 1.9 copy-start.4
  496.2 1.3 copy-start.2
  496.2 1.7 copy-start.5
  502.6 1.7 copy-start.13
  519.8 1.4 copy-start.1
  519.8 1.9 copy-start.4
  522.8 1.3 copy-start.2
  522.8 1.7 copy-start.5
  529.2 1.7 copy-start.13
  546.4 1.4 copy-start.1
  546.4 1.9 copy-start.4
  549.3 1.3 copy-start.2
  549.3 1.7 copy-start.5
  556.0 3.4 copy-start.3
  557.0 3.5 copy-start.16
  560.5 18.8 %reduce-scatter.35.cloned.1.call-start = ((), (), s32[]{:S(2)}) async-start(), calls=%async_computation.23 | async-start | bytes 589824
  565.9 24.5 %reduce-scatter.33.cloned.1.call-start = ((), (), s32[]{:S(2)}) async-start(), calls=%async_computation.22 | async-start | bytes 589824
  566.9 34.7 %reduce-scatter.31.cloned.1.call-start = ((), (), s32[]{:S(2)}) async-start(), calls=%async_computation.21 | async-start | bytes 589824
  568.0 46.2 %reduce-scatter.29.cloned.1.call-start = ((), (), s32[]{:S(2)}) async-start(), calls=%async_computation.20 | async-start | bytes 1769472 | tf_op jit(solution)/shard_map/reduce_scatter | solution.py:325
  574.6 39.7 %copy-start.19 = (bf16[2048,192]{0,1:T(8,128)(2,1)S(1)}, bf16[2048,192]{0,1:T(8,128)(2,1)}, u32[]{:S(2)}) copy-start(bf16[2048,192]{0,1:T(8,128)(2,1)} %convert.16) | copy-start | bytes 2359300
  574.6 39.7 %copy-start.20 = (bf16[2048,192]{0,1:T(8,128)(2,1)S(1)}, bf16[2048,192]{0,1:T(8,128)(2,1)}, u32[]{:S(2)}) copy-start(bf16[2048,192]{0,1:T(8,128)(2,1)} %convert.17) | copy-start | bytes 2359300
  574.6 120.0 %all-reduce.5.cloned.1.call-start = ((), (), s32[]{:S(2)}) async-start(), calls=%async_computation.26 | async-start | bytes 3538944 | tf_op jit(solution)/shard_map/psum | solution.py:338
  614.2 126.3 %reduce-scatter.27.cloned.1.call-start = ((), (), s32[]{:S(2)}) async-start(), calls=%async_computation.19 | async-start | bytes 3932160 | tf_op jit(solution)/shard_map/reduce_scatter | solution.py:17
  619.5 46.2 %copy-start.33 = (f32[768]{0:T(1024)S(1)}, f32[768]{0:T(1024)}, u32[]{:S(2)}) copy-start(f32[768]{0:T(1024)} %get-tuple-element.365) | copy-start | bytes 9220
  694.6 8.9 %copy-start.24 = (bf16[768,384]{1,0:T(8,128)(2,1)S(1)}, bf16[768,384]{1,0:T(8,128)(2,1)}, u32[]{:S(2)}) copy-start(bf16[768,384]{1,0:T(8,128)(2,1)} %get-tuple-element.327) | copy-start | bytes 1769476
  696.3 44.2 %copy-start.15 = (f32[512,768]{1,0:T(8,128)S(1)}, f32[512,768]{1,0:T(8,128)}, u32[]{:S(2)}) copy-start(f32[512,768]{1,0:T(8,128)} %get-tuple-element.333) | copy-start | bytes 4718596
  (11 other events, 8.4 us)
Sparse Core Ops, SparseCore 0:
  10.7 46.6 all-gather.6
  123.7 43.9 reduce-scatter.20
  287.5 43.9 all-gather.14
  395.7 43.9 all-gather.16
  614.3 80.2 all-reduce.4
  697.7 42.7 reduce-scatter.26
Sparse Core Ops, SparseCore 1:
  125.5 9.1 all-gather.10
  172.3 43.7 all-gather.8
  217.5 9.1 all-gather.12
  233.2 45.0 reduce-scatter.22
  345.4 43.8 reduce-scatter.24
  402.7 8.6 reduce-scatter.38
  560.6 7.7 reduce-scatter.36
  570.4 8.8 reduce-scatter.34
  581.5 8.8 reduce-scatter.32
  592.7 8.8 reduce-scatter.30
  604.4 9.7 reduce-scatter.28
where the time goes:
time: 756 us; the launch traced here: 752 us
  waiting for transfers between devices  377 us (50%)
  matrix products  177 us (23%)
  blocking collectives  69.3 us (9%)
  other arithmetic  62.3 us (8%)
  local copies, waits for them, and re-layouts  39.4 us (5%)
  between operations  19 us (3%)
    reduce_scatter x4, waiting for transfers between devices, sum_rows(): lax.psum_scatter(term_fn(jnp.int32(0), lax.axis_size('gz') * row_count).a...  167 us
    all_gather x4, waiting for transfers between devices, gather_rows(): return lax.all_gather(tensor, 'gz', axis=0, tiled=True)  162 us
    dot_general x24, matrix products, one_block(): jnp.einsum('qd,kd->qk', query_block[:, columns], key_rows[:, columns], pr...  50.6 us
    psum x1, blocking collectives, shards(): lax.psum((d_norm1_gain, d_norm1_bias, d_norm2_gain, d_norm2_bias, d_b_out...  43.8 us
    unnamed x22, waiting for transfers between devices  21.5 us
    dot_general x12, matrix products, one_block(): jnp.einsum('qd,kd->qk', grad_block[:, columns], value_rows[:, columns], p...  19.6 us
    unnamed x88, local copies, waits for them, and re-layouts  18.3 us
    psum x1, blocking collectives, shards(): lax.psum((d_bias_qkv[:col_width], d_bias_qkv[2 * col_width:], d_bias_up),...  16.3 us
  transfers between devices with their start and end apart: 17, of which 14 were waited for; matrix products, arithmetic and copies ran while one was open for 23% of the time, Pallas kernels for 0%

commit v1 on v0

--- a/solution.py
+++ b/solution.py
@@ -9,8 +9,30 @@
 EPSILON = 1e-05
 
 
+def in_order(blocks, dim):
+    shape = list(blocks.shape[1:])
+    shape[dim] *= blocks.shape[0]
+    return jnp.moveaxis(blocks, 0, dim).reshape(shape)
+
+
+def collect(x, axis, dim):
+    devices = lax.axis_size(axis)
+    pairs = [(i, (i + 1) % devices) for i in range(devices)]
+    back = [(b, a) for a, b in pairs]
+    lower, upper = ([], [])
+    for lap in range(devices - 1):
+        if lap % 2 == 0:
+            lower.append(lax.ppermute(lower[-1] if lower else x, axis, pairs))
+        else:
+            upper.append(lax.ppermute(upper[-1] if upper else x, axis, back))
+    parts = jnp.stack([*lower[::-1], x, *upper])
+    shift = lax.axis_index(axis) - len(lower)
+    parts = parts[(jnp.arange(devices) - shift) % devices]
+    return in_order(parts, dim)
+
+
 def gather_rows(tensor):
-    return lax.all_gather(tensor, "gz", axis=0, tiled=True)
+    return collect(tensor, "gz", 0)
 
 
 def sum_rows(term_fn, row_count):

time: 756 us -> 797 us (1.054)
  waiting for transfers between devices: 377 us -> 359 us
  local copies, waits for them, and re-layouts: 39.4 us -> 56.7 us
  starting transfers between devices: 1.12 us -> 16.6 us
  other arithmetic: 62.3 us -> 74.5 us
  matrix products: 177 us -> 188 us
    ppermute x0 -> x12, waiting for transfers between devices: none -> 184 us  [the longest x8 132 us: collect(): lower.append(lax.ppermute(lower[-1] if lower else x, axis, pairs))]
    all_gather x4 -> x0, waiting for transfers between devices: 162 us -> none  [gather_rows(): return lax.all_gather(tensor, 'gz', axis=0, tiled=True)]
    reduce_scatter x4, waiting for transfers between devices: 167 us -> 131 us  [sum_rows(): lax.psum_scatter(term_fn(jnp.int32(0), lax.axis_size('gz') * row_count).a...]
    gather x0 -> x4, local copies, waits for them, and re-layouts: none -> 17.4 us  [collect(): parts = parts[(jnp.arange(devices) - shift) % devices]]
    ppermute x0 -> x12, starting transfers between devices: none -> 15.8 us  [the longest x8 10.2 us: collect(): lower.append(lax.ppermute(lower[-1] if lower else x, axis, pairs))]
    another operation x2 -> x6, other arithmetic: 3.46 us -> 14.7 us  [the longest x4 11.3 us: collect(): parts = jnp.stack([*lower[::-1], x, *upper])]
    dot_general x24, matrix products: 50.6 us -> 61.5 us  [one_block(): jnp.einsum('qd,kd->qk', query_block[:, columns], key_rows[:, columns], pr...]
    unnamed x22 -> x18, waiting for transfers between devices: 21.5 us -> 19.9 us
  transfers between devices with their start and end apart: 17 -> 25, of which waited for: 14 -> 20; matrix products, arithmetic and copies ran while one was open for 23% -> 23% of each run, Pallas kernels for 0% -> 0%
where the time goes in v1:
time: 797 us; the launch traced here: 791 us
  waiting for transfers between devices  359 us (45%)
  matrix products  188 us (24%)
  other arithmetic  74.5 us (9%)
  blocking collectives  71.5 us (9%)
  local copies, waits for them, and re-layouts  56.7 us (7%)
  between operations  18.6 us (2%)
  starting transfers between devices  16.6 us (2%)
    ppermute x8, waiting for transfers between devices, collect(): lower.append(lax.ppermute(lower[-1] if lower else x, axis, pairs))  132 us
    reduce_scatter x4, waiting for transfers between devices, sum_rows(): lax.psum_scatter(term_fn(jnp.int32(0), lax.axis_size('gz') * row_count).a...  131 us
    dot_general x24, matrix products, one_block(): jnp.einsum('qd,kd->qk', query_block[:, columns], key_rows[:, columns], pr...  61.5 us
    ppermute x4, waiting for transfers between devices, collect(): upper.append(lax.ppermute(upper[-1] if upper else x, axis, back))  51.7 us
    psum x1, blocking collectives, shards(): lax.psum((d_norm1_gain, d_norm1_bias, d_norm2_gain, d_norm2_bias, d_b_out...  45.2 us
    unnamed x18, waiting for transfers between devices  19.9 us
    dot_general x12, matrix products, one_block(): jnp.einsum('qd,kd->qk', grad_block[:, columns], value_rows[:, columns], p...  19.3 us
    unnamed x86, local copies, waits for them, and re-layouts  17.8 us
  transfers between devices with their start and end apart: 25, of which 20 were waited for; matrix products, arithmetic and copies ran while one was open for 23% of the time, Pallas kernels for 0%

profile of v1, /device:TPU:0, one launch (start us, length us, event | category | flops | bytes accessed | tf_op | source)
XLA Modules:
  0.0 791.3 jit_solution(12361567323748329941)
XLA Ops:
  8.1 3.0 collective-permute-start
  16.7 13.9 %collective-permute-done = bf16[512,768]{1,0:T(8,128)(2,1)S(1)} collective-permute-done((bf16[512,768]{1,0:T(8,128)(2,1)}, bf16[512,768]{1,0:T(8,128)(2,1)S(1)}, u32[]{:S(2)}, u32[]{:S(2)}) %collective-permute-start) | collective-permute-done | bytes 786464 | tf_op jit(solution)/shard_map/ppermute | solution.py:25
  37.8 10.3 %collective-permute-done.2 = bf16[512,768]{1,0:T(8,128)(2,1)} collective-permute-done((bf16[512,768]{1,0:T(8,128)(2,1)}, bf16[512,768]{1,0:T(8,128)(2,1)}, u32[]{:S(2)}, u32[]{:S(2)}) %collective-permute-start.2) | collective-permute-done | bytes 786464 | tf_op jit(solution)/shard_map/ppermute | solution.py:27
  48.1 15.5 %collective-permute-done.1 = bf16[512,768]{1,0:T(8,128)(2,1)} collective-permute-done((bf16[512,768]{1,0:T(8,128)(2,1)S(1)}, bf16[512,768]{1,0:T(8,128)(2,1)}, u32[]{:S(2)}, u32[]{:S(2)}) %collective-permute-start.1) | collective-permute-done | bytes 786464 | tf_op jit(solution)/shard_map/ppermute | solution.py:25
  63.6 3.0 pad_maximum_fusion
  66.6 4.4 gather_fusion
  71.0 3.9 add_convert_fusion
  81.3 63.2 %while.27 = (s32[]{:T(128)}, bf16[4,512,192]{1,2,0:T(8,128)(2,1)}, f32[4,512,3]{1,2,0:T(4,128)S(1)}, s32[4]{0:T(128)S(1)}, s32[2048]{0:T(1024)S(1)}, /*index=5*/...) while((s32[]{:T(128)}, bf16[4,512,192]{1,2,0:T(8,128)(2,1)}, ...), condition=%wide.region_7.8_spmd, body=%wide.region_0.7_spmd.sunk | while | flops 843649024 | bytes 42000656 | solution.py:115
  82.9 2.8 fusion.160
  87.6 2.7 fusion.157
  92.1 2.7 fusion.163
  98.6 2.8 fusion.160
  103.3 2.7 fusion.157
  107.8 2.7 fusion.163
  114.4 2.8 fusion.160
  119.1 2.7 fusion.157
  123.6 2.7 fusion.163
  130.2 2.8 fusion.160
  134.9 2.7 fusion.157
  139.3 2.7 fusion.163
  145.8 2.7 convolution_convert_fusion.3
  149.2 44.0 %reduce-scatter.21.cloned.1.call-done = bf16[512,768]{1,0:T(8,128)(2,1)} async-done(((bf16[2048,768]{1,0:T(8,128)(2,1)}), bf16[512,768]{1,0:T(8,128)(2,1)}) %reduce-scatter.21.cloned.1.call-update) | async-done | bytes 786448 | tf_op jit(solution)/shard_map/reduce_scatter | solution.py:39
  200.7 18.6 %collective-permute-done.3 = bf16[512,768]{1,0:T(8,128)(2,1)} collective-permute-done((bf16[512,768]{1,0:T(8,128)(2,1)}, bf16[512,768]{1,0:T(8,128)(2,1)}, u32[]{:S(2)}, u32[]{:S(2)}) %collective-permute-start.3) | collective-permute-done | bytes 786464 | tf_op jit(solution)/shard_map/ppermute | solution.py:25
  219.9 16.2 %collective-permute-done.5 = bf16[512,768]{1,0:T(8,128)(2,1)} collective-permute-done((bf16[512,768]{1,0:T(8,128)(2,1)}, bf16[512,768]{1,0:T(8,128)(2,1)}, u32[]{:S(2)}, u32[]{:S(2)}) %collective-permute-start.5) | collective-permute-done | bytes 786464 | tf_op jit(solution)/shard_map/ppermute | solution.py:27
  236.1 15.8 %collective-permute-done.4 = bf16[512,768]{1,0:T(8,128)(2,1)} collective-permute-done((bf16[512,768]{1,0:T(8,128)(2,1)}, bf16[512,768]{1,0:T(8,128)(2,1)}, u32[]{:S(2)}, u32[]{:S(2)}) %collective-permute-start.4) | collective-permute-done | bytes 786464 | tf_op jit(solution)/shard_map/ppermute | solution.py:25
  251.9 3.2 pad_maximum_fusion.1
  255.1 4.3 gather_fusion.1
  259.4 7.0 multiply_convert_fusion.3
  266.3 6.5 convolution_convert_fusion.1
  274.1 42.7 %reduce-scatter.23.cloned.1.call-done = bf16[512,768]{1,0:T(8,128)(2,1)} async-done(((bf16[2048,768]{1,0:T(8,128)(2,1)}), bf16[512,768]{1,0:T(8,128)(2,1)}) %reduce-scatter.23.cloned.1.call-update) | async-done | bytes 786448 | tf_op jit(solution)/shard_map/reduce_scatter | solution.py:39
  321.4 2.9 fusion.73
  324.3 2.8 convert_reduce_fusion.2
  330.1 18.4 %collective-permute-done.6 = bf16[512,768]{1,0:T(8,128)(2,1)S(1)} collective-permute-done((bf16[512,768]{1,0:T(8,128)(2,1)S(1)}, bf16[512,768]{1,0:T(8,128)(2,1)S(1)}, u32[]{:S(2)}, u32[]{:S(2)}) %collective-permute-start.6) | collective-permute-done | bytes 786464 | tf_op jit(solution)/shard_map/ppermute | solution.py:25
  349.3 15.9 %collective-permute-done.8 = bf16[512,768]{1,0:T(8,128)(2,1)S(1)} collective-permute-done((bf16[512,768]{1,0:T(8,128)(2,1)S(1)}, bf16[512,768]{1,0:T(8,128)(2,1)S(1)}, u32[]{:S(2)}, u32[]{:S(2)}) %collective-permute-start.8) | collective-permute-done | bytes 786464 | tf_op jit(solution)/shard_map/ppermute | solution.py:27
  365.3 15.8 %collective-permute-done.7 = bf16[512,768]{1,0:T(8,128)(2,1)S(1)} collective-permute-done((bf16[512,768]{1,0:T(8,128)(2,1)S(1)}, bf16[512,768]{1,0:T(8,128)(2,1)S(1)}, u32[]{:S(2)}, u32[]{:S(2)}) %collective-permute-start.7) | collective-permute-done | bytes 786464 | tf_op jit(solution)/shard_map/ppermute | solution.py:25
  382.9 4.3 gather_fusion.2
  387.2 8.1 %convert_reduce_fusion = (f32[768]{0:T(1024)}, bf16[2048,768]{1,0:T(8,128)(2,1)S(1)}) fusion(f32[2048,768]{1,0:T(8,128)} %get-tuple-element.364, f32[768]{0:T(1024)S(1)} %convert_element_type.204, bf16[2048,768]{1,0:T(8,128)(2,1)} %bitcast.140, bf16[768,768]{1,0:T(8,128)(2,1)} %all-gather.5.cloned.1.call-done), kind=kOutput, calls=%fused_computation.107 | convolution fusion | flops 2436365568 | bytes 13768704 | tf_op jit(solution)/shard_map/lm,fm->lf/dot_general | solution.py:293
  397.0 4.0 convolution_convert_fusion
  401.1 44.0 %reduce-scatter.25.cloned.1.call-done = bf16[512,768]{1,0:T(8,128)(2,1)} async-done(((bf16[2048,768]{1,0:T(8,128)(2,1)}), bf16[512,768]{1,0:T(8,128)(2,1)}) %reduce-scatter.25.cloned.1.call-update) | async-done | bytes 786448 | tf_op jit(solution)/shard_map/reduce_scatter | solution.py:39
  445.0 3.5 multiply_reduce_fusion.4
  448.6 2.8 convert_reduce_fusion.3
  454.3 18.7 %collective-permute-done.9 = bf16[512,768]{1,0:T(8,128)(2,1)} collective-permute-done((bf16[512,768]{1,0:T(8,128)(2,1)}, bf16[512,768]{1,0:T(8,128)(2,1)}, u32[]{:S(2)}, u32[]{:S(2)}) %collective-permute-start.9) | collective-permute-done | bytes 786464 | tf_op jit(solution)/shard_map/ppermute | solution.py:25
  473.5 5.5 convolution_convert_fusion.5
  480.5 9.2 %collective-permute-done.11 = bf16[512,768]{1,0:T(8,128)(2,1)} collective-permute-done((bf16[512,768]{1,0:T(8,128)(2,1)}, bf16[512,768]{1,0:T(8,128)(2,1)}, u32[]{:S(2)}, u32[]{:S(2)}) %collective-permute-start.11) | collective-permute-done | bytes 786464 | tf_op jit(solution)/shard_map/ppermute | solution.py:27
  489.8 15.8 %collective-permute-done.10 = bf16[512,768]{1,0:T(8,128)(2,1)} collective-permute-done((bf16[512,768]{1,0:T(8,128)(2,1)}, bf16[512,768]{1,0:T(8,128)(2,1)}, u32[]{:S(2)}, u32[]{:S(2)}) %collective-permute-start.10) | collective-permute-done | bytes 786464 | tf_op jit(solution)/shard_map/ppermute | solution.py:25
  505.5 3.2 pad_maximum_fusion.3
  508.8 4.4 gather_fusion.3
  513.2 4.0 convolution_convert_fusion.4
  518.2 106.1 %while.28 = (s32[]{:T(128)}, f32[2048,192]{0,1:T(8,128)}, f32[2048,192]{0,1:T(8,128)}, bf16[4,512,192]{1,2,0:T(8,128)(2,1)}, s32[4]{0:T(128)S(1)}, /*index=5*/s3...) while((s32[]{:T(128)}, f32[2048,192]{0,1:T(8,128)}, ...), condition=%wide.region_27.28_spmd.clone, body=%wide.region_23.27_spmd.clone.sunk | while | flops 2058486784 | bytes 138699280 | solution.py:184
  530.1 2.5 multiply_reduce_fusion.15
  556.5 2.5 multiply_reduce_fusion.15
  583.0 2.5 multiply_reduce_fusion.15
  609.4 2.5 multiply_reduce_fusion.15
  625.5 2.9 fusion.66
  629.4 2.4 convert.16
  632.9 4.4 convolution_convert_fusion.7
  640.4 6.5 convolution_convert_fusion.6
  653.5 9.5 %reduce-scatter.33.cloned.1.call-done = bf16[384,192]{1,0:T(8,128)(2,1)} async-done(((bf16[768,192]{1,0:T(8,128)(2,1)}), bf16[384,192]{1,0:T(8,128)(2,1)}) %reduce-scatter.33.cloned.1.call-update) | async-done | bytes 147472
  664.8 9.3 %reduce-scatter.31.cloned.1.call-done = bf16[384,192]{1,0:T(8,128)(2,1)} async-done(((bf16[768,192]{1,0:T(8,128)(2,1)}), bf16[384,192]{1,0:T(8,128)(2,1)}) %reduce-scatter.31.cloned.1.call-update) | async-done | bytes 147472
  675.8 10.8 %reduce-scatter.29.cloned.1.call-done = bf16[384,768]{1,0:T(8,128)(2,1)} async-done(((bf16[768,768]{1,0:T(8,128)(2,1)}), bf16[384,768]{1,0:T(8,128)(2,1)}) %reduce-scatter.29.cloned.1.call-update) | async-done | bytes 589840 | tf_op jit(solution)/shard_map/reduce_scatter | solution.py:347
  686.7 5.2 convolution_convert_fusion.2
  692.7 45.2 %all-reduce = (f32[]{:T(128)}, f32[]{:T(128)}, f32[768]{0:T(1024)}, f32[768]{0:T(1024)}, f32[768]{0:T(1024)}, /*index=5*/f32[768]{0:T(1024)}, f32[768]{0:T(1024)}, f32[768]{0:T(1024)}) all-reduce(f32[]{:T(128)} %get-tuple-element.262, f32[]{:T(128)} %get-tuple-element.334, ...), channel_id=1, replica_groups=mesh['gx'=4,'gy'=2,'gz'=4] {'gx','gy','gz'}, use_global_device_ids=true, to_apply=%region_15.16 | all-reduce | flops 4610 | bytes 36880 | tf_op jit(solution)/shard_map/psum | solution.py:379
  739.7 17.2 %all-reduce.1 = (f32[192]{0:T(256)}, f32[192]{0:T(256)}, f32[768]{0:T(1024)}) all-reduce(f32[192]{0:T(256)S(1)} %get-tuple-element.362, f32[192]{0:T(256)S(1)} %get-tuple-element.361, f32[768]{0:T(1024)S(1)} %copy-done.31), channel_id=1, replica_groups=mesh['gx'=4,'gy'=2,'gz'=4] {'gx','gy'}, use_global_device_ids=true, to_apply=%region_32.33 | all-reduce | flops 1152 | bytes 9216 | tf_op jit(solution)/shard_map/psum | solution.py:367
  756.8 13.7 %all-reduce.5.cloned.1.call-done = (bf16[384,192]{0,1:T(8,128)(2,1)}, bf16[384,192]{0,1:T(8,128)(2,1)}, bf16[384,192]{0,1:T(8,128)(2,1)}, bf16[192,384]{1,0:T(8,...) async-done(((bf16[384,192]{0,1:T(8,128)(2,1)}, bf16[384,192]{0,1:T(8,128)(2,1)}, bf16[384,192]{0,1:T(8,128)(2,1)}, bf16[192,384]{1,0:T(8,128)(2,1)}, ...) | async-done | bytes 1769488 | tf_op jit(solution)/shard_map/psum | solution.py:360
  (373 shorter events, 198.2 us)
Async XLA Ops:
  8.0 55.6 %copy-start = (bf16[512,768]{1,0:T(8,128)(2,1)S(1)}, bf16[512,768]{1,0:T(8,128)(2,1)}, u32[]{:S(2)}) copy-start(bf16[512,768]{1,0:T(8,128)(2,1)} %param.24) | copy-start | bytes 2359300
  8.0 185.2 %reduce-scatter.21.cloned.1.call-start = ((), (), s32[]{:S(2)}) async-start(), calls=%async_computation.10 | async-start | bytes 3932160 | tf_op jit(solution)/shard_map/reduce_scatter | solution.py:39
  8.1 22.5 %collective-permute-start = (bf16[512,768]{1,0:T(8,128)(2,1)}, bf16[512,768]{1,0:T(8,128)(2,1)S(1)}, u32[]{:S(2)}, u32[]{:S(2)}) collective-permute-start(bf16[512,768]{1,0:T(8,128)(2,1)} %param.24), channel_id=1, source_target_pairs={{0,1},{1,2},{2,3},{3,0},{4,5},{5,6},{6,7},{7,4},{8,9},{9,10},{10,1... | collective-permute-start | bytes 2359304 | tf_op jit(solution)/shard_map/ppermute | solution.py:25
  11.1 37.1 %collective-permute-start.2 = (bf16[512,768]{1,0:T(8,128)(2,1)}, bf16[512,768]{1,0:T(8,128)(2,1)}, u32[]{:S(2)}, u32[]{:S(2)}) collective-permute-start(bf16[512,768]{1,0:T(8,128)(2,1)} %param.24), channel_id=1, source_target_pairs={{1,0},{2,1},{3,2},{0,3},{5,4},{6,5},{7,6},{4,7},{9,8},{10,9},{11,1... | collective-permute-start | bytes 2359304 | tf_op jit(solution)/shard_map/ppermute | solution.py:27
  14.4 131.4 %copy-start.18 = (bf16[192,768]{1,0:T(8,128)(2,1)}, bf16[192,768]{1,0:T(8,128)(2,1)S(1)}, u32[]{:S(2)}) copy-start(bf16[192,768]{1,0:T(8,128)(2,1)S(1)} %all_gather.21) | copy-start | bytes 884740
  30.6 33.0 %collective-permute-start.1 = (bf16[512,768]{1,0:T(8,128)(2,1)S(1)}, bf16[512,768]{1,0:T(8,128)(2,1)}, u32[]{:S(2)}, u32[]{:S(2)}) collective-permute-start(bf16[512,768]{1,0:T(8,128)(2,1)S(1)} %collective-permute-done), channel_id=1, source_target_pairs={{0,1},{1,2},{2,3},{3,0},{4,5},{5,6},{6,7},{7,4},{8,9},{9,10},{10,1... | collective-permute-start | bytes 2359304 | tf_op jit(solution)/shard_map/ppermute | solution.py:25
  37.8 25.8 %copy-start.22 = (bf16[768,576]{0,1:T(8,128)(2,1)}, bf16[768,576]{0,1:T(8,128)(2,1)S(1)}, u32[]{:S(2)}) copy-start(bf16[768,576]{0,1:T(8,128)(2,1)S(1)} %constant_dynamic-update-slice_fusion) | copy-start | bytes 2654212
  66.6 4.4 copy-start.23
  76.2 5.1 copy-start.20
  76.2 5.1 copy-start.24
  148.5 110.8 %all-gather.3.cloned.1.call-start = ((), (), s32[]{:S(2)}) async-start(), calls=%async_computation.11 | async-start | bytes 1769472 | tf_op jit(solution)/shard_map/all_gather | solution.py:225
  149.2 70.7 %copy-start.35 = (bf16[768]{0:T(1024)(128)(2,1)S(1)}, bf16[768]{0:T(1024)(128)(2,1)}, u32[]{:S(2)}) copy-start(bf16[768]{0:T(1024)(128)(2,1)} %param.39) | copy-start | bytes 4612
  193.2 3.1 copy-start.6
  197.7 21.6 %collective-permute-start.3 = (bf16[512,768]{1,0:T(8,128)(2,1)}, bf16[512,768]{1,0:T(8,128)(2,1)}, u32[]{:S(2)}, u32[]{:S(2)}) collective-permute-start(bf16[512,768]{1,0:T(8,128)(2,1)} %fusion.64), channel_id=1, source_target_pairs={{0,1},{1,2},{2,3},{3,0},{4,5},{5,6},{6,7},{7,4},{8,9},{9,10},{10,1... | collective-permute-start | bytes 2359304 | tf_op jit(solution)/shard_map/ppermute | solution.py:25
  199.1 67.2 %all-gather.5.cloned.1.call-start = ((), (), s32[]{:S(2)}) async-start(), calls=%async_computation.12 | async-start | bytes 1769472 | tf_op jit(solution)/shard_map/all_gather | solution.py:229
  199.1 37.0 %collective-permute-start.5 = (bf16[512,768]{1,0:T(8,128)(2,1)}, bf16[512,768]{1,0:T(8,128)(2,1)}, u32[]{:S(2)}, u32[]{:S(2)}) collective-permute-start(bf16[512,768]{1,0:T(8,128)(2,1)} %fusion.64), channel_id=1, source_target_pairs={{1,0},{2,1},{3,2},{0,3},{5,4},{6,5},{7,6},{4,7},{9,8},{10,9},{11,1... | collective-permute-start | bytes 2359304 | tf_op jit(solution)/shard_map/ppermute | solution.py:27
  219.3 32.6 %collective-permute-start.4 = (bf16[512,768]{1,0:T(8,128)(2,1)}, bf16[512,768]{1,0:T(8,128)(2,1)}, u32[]{:S(2)}, u32[]{:S(2)}) collective-permute-start(bf16[512,768]{1,0:T(8,128)(2,1)} %collective-permute-done.3), channel_id=1, source_target_pairs={{0,1},{1,2},{2,3},{3,0},{4,5},{5,6},{6,7},{7,4},{8,9},{9,10},{10,1... | collective-permute-start | bytes 2359304 | tf_op jit(solution)/shard_map/ppermute | solution.py:25
  219.8 97.0 %reduce-scatter.23.cloned.1.call-start = ((), (), s32[]{:S(2)}) async-start(), calls=%async_computation.13 | async-start | bytes 3932160 | tf_op jit(solution)/shard_map/reduce_scatter | solution.py:39
  272.9 172.2 %reduce-scatter.25.cloned.1.call-start = ((), (), s32[]{:S(2)}) async-start(), calls=%async_computation.14 | async-start | bytes 3932160 | tf_op jit(solution)/shard_map/reduce_scatter | solution.py:39
  316.9 4.5 copy-start.7
  316.9 4.5 copy-start.11
  316.9 4.5 copy-start.13
  316.9 4.5 copy-start.14
  327.1 21.3 %collective-permute-start.6 = (bf16[512,768]{1,0:T(8,128)(2,1)S(1)}, bf16[512,768]{1,0:T(8,128)(2,1)S(1)}, u32[]{:S(2)}, u32[]{:S(2)}) collective-permute-start(bf16[512,768]{1,0:T(8,128)(2,1)S(1)} %get-tuple-element.329), channel_id=1, source_target_pairs={{0,1},{1,2},{2,3},{3,0},{4,5},{5,6},{6,7},{7,4},{8,9},{9,10},{10,1... | collective-permute-start | bytes 2359304 | tf_op jit(solution)/shard_map/ppermute | solution.py:25
  328.5 36.7 %collective-permute-start.8 = (bf16[512,768]{1,0:T(8,128)(2,1)S(1)}, bf16[512,768]{1,0:T(8,128)(2,1)S(1)}, u32[]{:S(2)}, u32[]{:S(2)}) collective-permute-start(bf16[512,768]{1,0:T(8,128)(2,1)S(1)} %get-tuple-element.329), channel_id=1, source_target_pairs={{1,0},{2,1},{3,2},{0,3},{5,4},{6,5},{7,6},{4,7},{9,8},{10,9},{11,1... | collective-permute-start | bytes 2359304 | tf_op jit(solution)/shard_map/ppermute | solution.py:27
  348.5 32.6 %collective-permute-start.7 = (bf16[512,768]{1,0:T(8,128)(2,1)S(1)}, bf16[512,768]{1,0:T(8,128)(2,1)S(1)}, u32[]{:S(2)}, u32[]{:S(2)}) collective-permute-start(bf16[512,768]{1,0:T(8,128)(2,1)S(1)} %collective-permute-done.6), channel_id=1, source_target_pairs={{0,1},{1,2},{2,3},{3,0},{4,5},{5,6},{6,7},{7,4},{8,9},{9,10},{10,1... | collective-permute-start | bytes 2359304 | tf_op jit(solution)/shard_map/ppermute | solution.py:25
  387.2 9.7 %copy-start.39 = (bf16[768,768]{1,0:T(8,128)(2,1)S(1)}, bf16[768,768]{1,0:T(8,128)(2,1)}, u32[]{:S(2)}) copy-start(bf16[768,768]{1,0:T(8,128)(2,1)} %all-gather.3.cloned.1.call-done) | copy-start | bytes 3538948
  395.3 1.7 copy-start.40
  401.0 246.0 %reduce-scatter.39.cloned.1.call-start = ((), (), s32[]{:S(2)}) async-start(), calls=%async_computation.21 | async-start | bytes 1769472
  445.0 3.6 copy-start.8
  445.0 3.6 copy-start.9
  445.0 3.6 copy-start.17
  451.3 21.6 %collective-permute-start.9 = (bf16[512,768]{1,0:T(8,128)(2,1)}, bf16[512,768]{1,0:T(8,128)(2,1)}, u32[]{:S(2)}, u32[]{:S(2)}) collective-permute-start(bf16[512,768]{1,0:T(8,128)(2,1)} %get-tuple-element.332), channel_id=1, source_target_pairs={{0,1},{1,2},{2,3},{3,0},{4,5},{5,6},{6,7},{7,4},{8,9},{9,10},{10,1... | collective-permute-start | bytes 2359304 | tf_op jit(solution)/shard_map/ppermute | solution.py:25
  452.7 37.0 %collective-permute-start.11 = (bf16[512,768]{1,0:T(8,128)(2,1)}, bf16[512,768]{1,0:T(8,128)(2,1)}, u32[]{:S(2)}, u32[]{:S(2)}) collective-permute-start(bf16[512,768]{1,0:T(8,128)(2,1)} %get-tuple-element.332), channel_id=1, source_target_pairs={{1,0},{2,1},{3,2},{0,3},{5,4},{6,5},{7,6},{4,7},{9,8},{10,9},{11,1... | collective-permute-start | bytes 2359304 | tf_op jit(solution)/shard_map/ppermute | solution.py:27
  473.0 32.6 %collective-permute-start.10 = (bf16[512,768]{1,0:T(8,128)(2,1)}, bf16[512,768]{1,0:T(8,128)(2,1)}, u32[]{:S(2)}, u32[]{:S(2)}) collective-permute-start(bf16[512,768]{1,0:T(8,128)(2,1)} %collective-permute-done.9), channel_id=1, source_target_pairs={{0,1},{1,2},{2,3},{3,0},{4,5},{5,6},{6,7},{7,4},{8,9},{9,10},{10,1... | collective-permute-start | bytes 2359304 | tf_op jit(solution)/shard_map/ppermute | solution.py:25
  480.5 168.7 %reduce-scatter.37.cloned.1.call-start = ((), (), s32[]{:S(2)}) async-start(), calls=%async_computation.20 | async-start | bytes 589824
  508.8 4.4 copy-start.19
  513.2 5.0 copy-start.10
  540.1 1.4 copy-start.1
  540.1 1.9 copy-start.4
  543.0 1.7 copy-start.5
  566.5 1.4 copy-start.1
  566.5 1.9 copy-start.4
  569.5 1.3 copy-start.2
  569.5 1.7 copy-start.5
  593.0 1.4 copy-start.1
  593.0 1.9 copy-start.4
  596.0 1.7 copy-start.5
  619.4 1.4 copy-start.1
  619.4 1.9 copy-start.4
  622.4 1.3 copy-start.2
  622.4 1.7 copy-start.5
  628.5 3.4 copy-start.3
  632.9 18.9 %reduce-scatter.35.cloned.1.call-start = ((), (), s32[]{:S(2)}) async-start(), calls=%async_computation.19 | async-start | bytes 589824
  638.3 24.8 %reduce-scatter.33.cloned.1.call-start = ((), (), s32[]{:S(2)}) async-start(), calls=%async_computation.18 | async-start | bytes 589824
  639.3 34.8 %reduce-scatter.31.cloned.1.call-start = ((), (), s32[]{:S(2)}) async-start(), calls=%async_computation.17 | async-start | bytes 589824
  640.3 46.3 %reduce-scatter.29.cloned.1.call-start = ((), (), s32[]{:S(2)}) async-start(), calls=%async_computation.16 | async-start | bytes 1769472 | tf_op jit(solution)/shard_map/reduce_scatter | solution.py:347
  646.9 39.8 %copy-start.15 = (bf16[2048,192]{0,1:T(8,128)(2,1)S(1)}, bf16[2048,192]{0,1:T(8,128)(2,1)}, u32[]{:S(2)}) copy-start(bf16[2048,192]{0,1:T(8,128)(2,1)} %convert.16) | copy-start | bytes 2359300
  646.9 39.8 %copy-start.16 = (bf16[2048,192]{0,1:T(8,128)(2,1)S(1)}, bf16[2048,192]{0,1:T(8,128)(2,1)}, u32[]{:S(2)}) copy-start(bf16[2048,192]{0,1:T(8,128)(2,1)} %convert.17) | copy-start | bytes 2359300
  646.9 123.6 %all-reduce.5.cloned.1.call-start = ((), (), s32[]{:S(2)}) async-start(), calls=%async_computation.22 | async-start | bytes 3538944 | tf_op jit(solution)/shard_map/psum | solution.py:360
  686.7 93.8 %reduce-scatter.27.cloned.1.call-start = ((), (), s32[]{:S(2)}) async-start(), calls=%async_computation.15 | async-start | bytes 3932160 | tf_op jit(solution)/shard_map/reduce_scatter | solution.py:39
  692.0 47.7 %copy-start.31 = (f32[768]{0:T(1024)S(1)}, f32[768]{0:T(1024)}, u32[]{:S(2)}) copy-start(f32[768]{0:T(1024)} %get-tuple-element.365) | copy-start | bytes 9220
  739.6 40.8 %copy-start.12 = (f32[512,768]{1,0:T(8,128)S(1)}, f32[512,768]{1,0:T(8,128)}, u32[]{:S(2)}) copy-start(f32[512,768]{1,0:T(8,128)} %get-tuple-element.333) | copy-start | bytes 4718596
  770.5 8.8 %copy-start.21 = (bf16[768,384]{1,0:T(8,128)(2,1)S(1)}, bf16[768,384]{1,0:T(8,128)(2,1)}, u32[]{:S(2)}) copy-start(bf16[768,384]{1,0:T(8,128)(2,1)} %get-tuple-element.327) | copy-start | bytes 1769476
  (14 other events, 11.0 us)
Sparse Core Ops, SparseCore 0:
  148.7 44.4 reduce-scatter.20
  273.0 43.8 reduce-scatter.22
  401.1 43.8 reduce-scatter.24
  692.1 45.9 reduce-scatter.26
Sparse Core Ops, SparseCore 1:
  199.2 9.2 all-gather.2
  219.9 10.0 all-gather.4
  480.6 9.5 reduce-scatter.38
  633.0 7.6 reduce-scatter.36
  642.9 8.8 reduce-scatter.34
  654.2 8.8 reduce-scatter.32
  665.2 8.8 reduce-scatter.30
  676.9 9.7 reduce-scatter.28
  690.5 80.0 all-reduce.4
